TPU v7x, 32 devices: a whole 2x2x4 slice. The times are simulated.
32 devices in a mesh: dp: 8 (over z, core), mp: 4 (over y, x).
Axes of the slice: x: 2, y: 2, z: 4, core: 2. Of those that a mesh axis runs over, the one named last changes fastest.
Arguments:
- momentum: float32 [8, 256, 5120], P('dp', 'mp'), may hold values from -60 to 60
- gradient: bfloat16 [8, 256, 5120], P('dp', 'mp'), may hold values from -60 to 60
- columns: int32 [256], replicated, may hold values from 0 to 5119, as said below
Outputs:
- update: bfloat16 [256, 5120], P('mp', 'dp')
- new_momentum: float32 [8, 256, 5120], P('dp', 'mp')
Inputs may be any that keep to these rules, and one draw needn't show every extreme that they name: `columns`: 256 distinct frequencies, 0 and 5119 always among them, in no particular order.
All inputs are finite; a program needn't handle non-finite values.
Results may differ from a plain program's by a relative error of at most 0.007.
Values may be sent and summed in bfloat16 or wider, within the bound.
A program may use at most 64 MiB of HBM per device.

v0:
```python
import math
import jax
import jax.numpy as jnp
from jax import lax
from jax.sharding import PartitionSpec as P

COLS = 5120
RANK = 256
ITERS = 5
inertia = 0.9
linear_term = 3.4445
cubic_term = -4.775
quintic_term = 2.0315


def dct_table(columns):
    positions = jnp.arange(COLS, dtype=jnp.int32)
    phase_index = (2 * positions[:, None] + 1) * columns[None, :] % (4 * COLS)
    angles = phase_index.astype(jnp.float32) * (math.pi / (2 * COLS))
    column_scale = jnp.where(columns == 0, math.sqrt(1.0 / COLS), math.sqrt(2.0 / COLS))
    return (jnp.cos(angles) * column_scale[None, :]).astype(jnp.bfloat16)


def orthogonalize(gram_matrix):
    squared_norm = jnp.trace(gram_matrix) + 1e-06
    inverse_norm = 1.0 / jnp.sqrt(squared_norm)
    identity = jnp.eye(gram_matrix.shape[0], dtype=jnp.float32)
    gram_now = gram_matrix * (inverse_norm * inverse_norm)
    mixing = identity * inverse_norm
    highest = lax.Precision.HIGHEST
    for _ in range(ITERS):
        polynomial = (
            linear_term * identity
            + cubic_term * gram_now
            + quintic_term * jnp.dot(gram_now, gram_now, precision=highest)
        )
        mixing = jnp.dot(mixing, polynomial, precision=highest)
        gram_now = jnp.dot(
            jnp.dot(polynomial, gram_now, precision=highest), polynomial, precision=highest
        )
    return mixing


def body(momentum, gradient, columns):
    highest = lax.Precision.HIGHEST
    cosines = dct_table(columns)
    current = inertia * momentum[0] + gradient[0].astype(jnp.float32)
    partial_value = jnp.dot(
        current.astype(jnp.bfloat16), cosines, preferred_element_type=jnp.float32
    )
    replica_count = lax.axis_size("dp")
    summed = lax.psum(partial_value, "dp") / replica_count
    coded_rows = summed.astype(jnp.bfloat16)
    block_rows = lax.all_gather(summed, "mp", axis=0, tiled=True)
    gram_matrix = jnp.dot(block_rows.T, block_rows, precision=highest)
    mixing = orthogonalize(gram_matrix)
    orthogonal = jnp.dot(summed, mixing, precision=highest).astype(jnp.bfloat16)
    decoded = jnp.dot(coded_rows, cosines.T, preferred_element_type=jnp.float32)
    band_width = COLS // replica_count
    band_start = lax.axis_index("dp") * band_width
    band_cosines = lax.dynamic_slice_in_dim(cosines, band_start, band_width, 0)
    direction = jnp.dot(orthogonal, band_cosines.T, preferred_element_type=jnp.float32)
    row_count = momentum.shape[1] * lax.axis_size("mp")
    update = (direction * math.sqrt(row_count * COLS / RANK)).astype(jnp.bfloat16)
    new_momentum = (current - decoded)[None]
    return (update, new_momentum)


def solution(mesh):
    return jax.shard_map(
        body,
        mesh=mesh,
        in_specs=(P("dp", "mp", None), P("dp", "mp", None), P()),
        out_specs=(P("mp", "dp"), P("dp", "mp", None)),
        check_vma=False,
    )
```

profile of v0, /device:TPU:0, one launch (start us, length us, event | category | flops | bytes accessed | tf_op | source)
XLA Modules:
  0.0 141.9 jit_solution(5607261184913191640)
XLA Ops:
  7.2 0.7 compare_select_fusion
  7.9 25.8 %fusion.15 = f32[64,256]{1,0:T(8,128)} fusion(bf16[1,64,5120]{2,1,0:T(8,128)(2,1)} %param.4, f32[1,64,5120]{2,1,0:T(8,128)} %param.3, f32[256]{0:T(256)S(1)} %compare_select_fusion, s32[256]{0:T(256)} %param.5, s32[5120]{0:T(1024)S(1)} %multiply_add_fusion), kind=kOutput, calls=%fused_computation.27 | convolution fusion | flops 183500800 | bytes 2054144 | tf_op jit(solution)/shard_map/dot_general | solution.py:48
  33.7 22.0 %fusion.5 = bf16[5120,256]{1,0:T(8,128)(2,1)S(1)} fusion(f32[256]{0:T(256)S(1)} %compare_select_fusion, s32[256]{0:T(256)S(1)} %copy-done.1, s32[5120]{0:T(1024)S(1)} %multiply_add_fusion), kind=kLoop, calls=%fused_computation.7 | loop fusion | flops 14417920 | bytes 2643968 | tf_op jit(solution)/shard_map/convert_element_type | solution.py:21
  55.8 35.5 %all-reduce.2.cloned.1.call-done = f32[64,256]{1,0:T(8,128)} async-done(((f32[64,256]{1,0:T(8,128)}), f32[64,256]{1,0:T(8,128)}) %all-reduce.2.cloned.1.call-update) | async-done | bytes 65552 | tf_op jit(solution)/shard_map/psum | solution.py:52
  91.3 0.8 broadcast_multiply_fusion
  92.1 9.5 %all_gather.3 = f32[256,256]{1,0:T(8,128)S(1)} all-gather(f32[64,256]{1,0:T(8,128)S(1)} %broadcast_multiply_fusion), channel_id=1, replica_groups=mesh['dp'=8,'mp'=4] {'mp'}, dimensions={0}, use_global_device_ids=true | all-gather | bytes 327680 | tf_op jit(solution)/shard_map/all_gather | solution.py:54
  101.6 1.2 select_reduce_fusion
  103.5 0.4 fusion.13
  103.9 0.4 fusion.21
  104.7 0.4 fusion.39
  105.1 0.4 fusion.12
  105.8 0.4 fusion.42
  106.2 0.4 fusion.11
  106.6 0.4 fusion.44
  107.0 0.4 fusion.45
  107.4 0.4 fusion.10
  107.8 0.4 fusion.47
  108.2 0.4 fusion.48
  108.6 0.4 fusion.9
  109.0 0.4 fusion.40
  109.4 0.4 fusion.43
  110.1 0.4 fusion.49
  110.8 0.9 fusion.14
  111.7 23.3 %fusion = f32[1,64,5120]{2,1,0:T(8,128)} fusion(bf16[1,64,5120]{2,1,0:T(8,128)(2,1)S(1)} %copy-done.3, f32[1,64,5120]{2,1,0:T(8,128)S(1)} %copy-done.2, f32[256]{0:T(256)S(1)} %compare_select_fusion, s32[256]{0:T(256)S(1)} %copy-done.1, s32[5120]{0:T(1024)S(1)} %multiply_add_fusion, f32[64,256]{1,0:T(8,128)S(1)} %copy-done), kind=kOutput, calls=%fused_computation.2 | convolution fusion | flops 183533568 | bytes 3364864 | tf_op jit(solution)/shard_map/dot_general | solution.py:58
  (15 shorter events, 1.5 us)
Async XLA Ops:
  7.2 84.1 %all-reduce.2.cloned.1.call-start = ((), (), s32[]{:S(2)}) async-start(), calls=%async_computation | async-start | bytes 131072 | tf_op jit(solution)/shard_map/psum | solution.py:52
  7.9 25.8 %copy-start.1 = (s32[256]{0:T(256)S(1)}, s32[256]{0:T(256)}, u32[]{:S(2)}) copy-start(s32[256]{0:T(256)} %param.5) | copy-start | bytes 3076
  107.8 2.7 %copy-start = (f32[64,256]{1,0:T(8,128)S(1)}, f32[64,256]{1,0:T(8,128)}, u32[]{:S(2)}) copy-start(f32[64,256]{1,0:T(8,128)} %all-reduce.2.cloned.1.call-done) | copy-start | bytes 196612
  108.2 3.5 %copy-start.2 = (f32[1,64,5120]{2,1,0:T(8,128)S(1)}, f32[1,64,5120]{2,1,0:T(8,128)}, u32[]{:S(2)}) copy-start(f32[1,64,5120]{2,1,0:T(8,128)} %param.3) | copy-start | bytes 3932164
  108.2 3.5 %copy-start.3 = (bf16[1,64,5120]{2,1,0:T(8,128)(2,1)S(1)}, bf16[1,64,5120]{2,1,0:T(8,128)(2,1)}, u32[]{:S(2)}) copy-start(bf16[1,64,5120]{2,1,0:T(8,128)(2,1)} %param.4) | copy-start | bytes 1966084
Sparse Core Ops, SparseCore 0:
  33.8 57.4 all-reduce.1
where the time goes:
time: 142 us
  matrix products  58.3 us (41%)
  waiting for transfers between devices  35.5 us (25%)
  other arithmetic  23.6 us (17%)
  between operations  14.9 us (10%)
  blocking collectives  9.46 us (7%)
    psum x1, waiting for transfers between devices, body(): summed = lax.psum(partial_value, 'dp') / replica_count  35.5 us
    dot_general x1, matrix products, body(): jnp.dot(current.astype(jnp.bfloat16), cosines, preferred_element_type=jnp...  25.8 us
    dot_general x1, matrix products, body(): decoded = jnp.dot(coded_rows, cosines.T, preferred_element_type=jnp.float32)  23.3 us
    convert_element_type x1, other arithmetic, dct_table(): return (jnp.cos(angles) * column_scale[None, :]).astype(jnp.bfloat16)  22 us
    all_gather x1, blocking collectives, body(): block_rows = lax.all_gather(summed, 'mp', axis=0, tiled=True)  9.46 us
  transfers between devices with their start and end apart: 1, of which 1 were waited for; matrix products, arithmetic and copies ran while one was open for 16% of the time, Pallas kernels for 0%

commit v1 on v0

--- a/solution.py
+++ b/solution.py
@@ -51,7 +51,16 @@
     replica_count = lax.axis_size("dp")
     summed = lax.psum(partial_value, "dp") / replica_count
     coded_rows = summed.astype(jnp.bfloat16)
-    block_rows = lax.all_gather(summed, "mp", axis=0, tiled=True)
+    size_here = jax.lax.psum(1, "mp")
+    built = sorted(((kk, (kk + 1) % size_here) for kk in range(size_here)))
+    seen_now = summed
+    queue = [seen_now]
+    for dev_i in [*range(1, size_here)]:
+        seen_now = jax.lax.ppermute(seen_now, "mp", built)
+        queue.insert(0, seen_now)
+    after = jnp.concatenate(queue, axis=0)
+    right_arr = jax.lax.axis_index("mp") + 1
+    block_rows = jnp.roll(after, right_arr * summed.shape[0], axis=0)
     gram_matrix = jnp.dot(block_rows.T, block_rows, precision=highest)
     mixing = orthogonalize(gram_matrix)
     orthogonal = jnp.dot(summed, mixing, precision=highest).astype(jnp.bfloat16)

time: 142 us -> 164 us (1.15)
  waiting for transfers between devices: 35.5 us -> 61.3 us
  blocking collectives: 9.46 us -> 0 us
  starting transfers between devices: 0.04 us -> 4.68 us
    psum x1, waiting for transfers between devices: 35.5 us -> 57.6 us  [body(): summed = lax.psum(partial_value, 'dp') / replica_count]
    all_gather x1 -> x0, blocking collectives: 9.46 us -> none  [body(): block_rows = lax.all_gather(summed, 'mp', axis=0, tiled=True)]
    ppermute x0 -> x3, starting transfers between devices: none -> 4.64 us  [body(): seen_now = jax.lax.ppermute(seen_now, 'mp', built)]
    ppermute x0 -> x3, waiting for transfers between devices: none -> 3.7 us  [body(): seen_now = jax.lax.ppermute(seen_now, 'mp', built)]
  transfers between devices with their start and end apart: 1 -> 4, of which waited for: 1 -> 2; matrix products, arithmetic and copies ran while one was open for 16% -> 28% of each run, Pallas kernels for 0% -> 0%
where the time goes in v1:
time: 164 us
  waiting for transfers between devices  61.3 us (37%)
  matrix products  59.2 us (36%)
  other arithmetic  23.6 us (14%)
  between operations  15 us (9%)
  starting transfers between devices  4.68 us (3%)
    psum x1, waiting for transfers between devices, body(): summed = lax.psum(partial_value, 'dp') / replica_count  57.6 us
    dot_general x1, matrix products, body(): jnp.dot(current.astype(jnp.bfloat16), cosines, preferred_element_type=jnp...  25.8 us
    dot_general x1, matrix products, body(): decoded = jnp.dot(coded_rows, cosines.T, preferred_element_type=jnp.float32)  24.3 us
    convert_element_type x1, other arithmetic, dct_table(): return (jnp.cos(angles) * column_scale[None, :]).astype(jnp.bfloat16)  22 us
    ppermute x3, starting transfers between devices, body(): seen_now = jax.lax.ppermute(seen_now, 'mp', built)  4.64 us
    ppermute x3, waiting for transfers between devices, body(): seen_now = jax.lax.ppermute(seen_now, 'mp', built)  3.7 us
  transfers between devices with their start and end apart: 4, of which 2 were waited for; matrix products, arithmetic and copies ran while one was open for 28% of the time, Pallas kernels for 0%

profile of v1, /device:TPU:0, one launch (start us, length us, event | category | flops | bytes accessed | tf_op | source)
XLA Modules:
  0.0 163.9 jit_solution(4000104963032374002)
XLA Ops:
  7.2 0.7 compare_select_fusion
  7.9 25.8 %fusion.15 = f32[64,256]{1,0:T(8,128)} fusion(bf16[1,64,5120]{2,1,0:T(8,128)(2,1)} %param.4, f32[1,64,5120]{2,1,0:T(8,128)} %param.3, f32[256]{0:T(256)S(1)} %compare_select_fusion, s32[256]{0:T(256)} %param.5, s32[5120]{0:T(1024)S(1)} %multiply_add_fusion), kind=kOutput, calls=%fused_computation.27 | convolution fusion | flops 183500800 | bytes 2054144 | tf_op jit(solution)/shard_map/dot_general | solution.py:48
  33.7 57.6 %all-reduce.2.cloned.1.call-done = f32[64,256]{1,0:T(8,128)} async-done(((f32[64,256]{1,0:T(8,128)}), f32[64,256]{1,0:T(8,128)}) %all-reduce.2.cloned.1.call-update) | async-done | bytes 65552 | tf_op jit(solution)/shard_map/psum | solution.py:52
  91.3 0.9 broadcast_multiply_fusion
  92.2 1.5 collective-permute-start
  93.7 3.7 %collective-permute-done = f32[64,256]{1,0:T(8,128)S(1)} collective-permute-done((f32[64,256]{1,0:T(8,128)S(1)}, f32[64,256]{1,0:T(8,128)S(1)}, u32[]{:S(2)}, u32[]{:S(2)}) %collective-permute-start) | collective-permute-done | bytes 65568 | tf_op jit(solution)/shard_map/ppermute | solution.py:59
  97.4 1.0 collective-permute-start.1
  98.4 22.0 %fusion.5 = bf16[5120,256]{1,0:T(8,128)(2,1)S(1)} fusion(f32[256]{0:T(256)S(1)} %compare_select_fusion, s32[256]{0:T(256)S(1)} %copy-done.1, s32[5120]{0:T(1024)S(1)} %multiply_add_fusion), kind=kLoop, calls=%fused_computation.7 | loop fusion | flops 14417920 | bytes 2643968 | tf_op jit(solution)/shard_map/convert_element_type | solution.py:21
  120.5 2.2 %collective-permute-start.2 = (f32[64,256]{1,0:T(8,128)S(1)}, f32[64,256]{1,0:T(8,128)S(1)}, u32[]{:S(2)}, u32[]{:S(2)}) collective-permute-start(f32[64,256]{1,0:T(8,128)S(1)} %collective-permute-done.1), channel_id=1, source_target_pairs={{0,1},{1,2},{2,3},{3,0},{4,5},{5,6},{6,7},{7,4},{8,9},{9,10},{10,1... | collective-permute-start | bytes 196616 | tf_op jit(solution)/shard_map/ppermute | solution.py:59
  122.6 24.3 %fusion = f32[1,64,5120]{2,1,0:T(8,128)} fusion(bf16[1,64,5120]{2,1,0:T(8,128)(2,1)S(1)} %copy-done.2, f32[1,64,5120]{2,1,0:T(8,128)} %param.3, f32[256]{0:T(256)S(1)} %compare_select_fusion, s32[256]{0:T(256)S(1)} %copy-done.1, s32[5120]{0:T(1024)S(1)} %multiply_add_fusion, f32[64,256]{1,0:T(8,128)S(1)} %copy-done), kind=kOutput, calls=%fused_computation.2 | convolution fusion | flops 183533568 | bytes 3364864 | tf_op jit(solution)/shard_map/dot_general | solution.py:67
  147.0 1.2 select_reduce_fusion
  148.9 0.4 fusion.13
  149.3 0.4 fusion.23
  150.5 0.4 fusion.12
  151.3 0.4 fusion.45
  152.0 0.4 fusion.47
  152.4 0.4 fusion.48
  153.2 0.4 fusion.50
  153.6 0.4 fusion.51
  154.4 0.4 fusion.43
  154.8 0.4 fusion.46
  155.1 0.4 fusion.49
  155.5 0.4 fusion.52
  156.2 0.9 fusion.14
  (26 shorter events, 2.7 us)
Async XLA Ops:
  7.2 84.1 %all-reduce.2.cloned.1.call-start = ((), (), s32[]{:S(2)}) async-start(), calls=%async_computation | async-start | bytes 131072 | tf_op jit(solution)/shard_map/psum | solution.py:52
  7.9 90.5 %copy-start.1 = (s32[256]{0:T(256)S(1)}, s32[256]{0:T(256)}, u32[]{:S(2)}) copy-start(s32[256]{0:T(256)} %param.5) | copy-start | bytes 3076
  33.7 88.9 %copy-start.2 = (bf16[1,64,5120]{2,1,0:T(8,128)(2,1)S(1)}, bf16[1,64,5120]{2,1,0:T(8,128)(2,1)}, u32[]{:S(2)}) copy-start(bf16[1,64,5120]{2,1,0:T(8,128)(2,1)} %param.4) | copy-start | bytes 1966084
  91.3 31.3 %copy-start = (f32[64,256]{1,0:T(8,128)S(1)}, f32[64,256]{1,0:T(8,128)}, u32[]{:S(2)}) copy-start(f32[64,256]{1,0:T(8,128)} %all-reduce.2.cloned.1.call-done) | copy-start | bytes 196612
  92.2 5.2 %collective-permute-start = (f32[64,256]{1,0:T(8,128)S(1)}, f32[64,256]{1,0:T(8,128)S(1)}, u32[]{:S(2)}, u32[]{:S(2)}) collective-permute-start(f32[64,256]{1,0:T(8,128)S(1)} %broadcast_multiply_fusion), channel_id=1, source_target_pairs={{0,1},{1,2},{2,3},{3,0},{4,5},{5,6},{6,7},{7,4},{8,9},{9,10},{10,1... | collective-permute-start | bytes 196616 | tf_op jit(solution)/shard_map/ppermute | solution.py:59
  97.4 23.1 %collective-permute-start.1 = (f32[64,256]{1,0:T(8,128)S(1)}, f32[64,256]{1,0:T(8,128)S(1)}, u32[]{:S(2)}, u32[]{:S(2)}) collective-permute-start(f32[64,256]{1,0:T(8,128)S(1)} %collective-permute-done), channel_id=1, source_target_pairs={{0,1},{1,2},{2,3},{3,0},{4,5},{5,6},{6,7},{7,4},{8,9},{9,10},{10,1... | collective-permute-start | bytes 196616 | tf_op jit(solution)/shard_map/ppermute | solution.py:59
  120.5 26.5 %collective-permute-start.2 = (f32[64,256]{1,0:T(8,128)S(1)}, f32[64,256]{1,0:T(8,128)S(1)}, u32[]{:S(2)}, u32[]{:S(2)}) collective-permute-start(f32[64,256]{1,0:T(8,128)S(1)} %collective-permute-done.1), channel_id=1, source_target_pairs={{0,1},{1,2},{2,3},{3,0},{4,5},{5,6},{6,7},{7,4},{8,9},{9,10},{10,1... | collective-permute-start | bytes 196616 | tf_op jit(solution)/shard_map/ppermute | solution.py:59
Sparse Core Ops, SparseCore 0:
  33.8 57.4 all-reduce.1
